TPU v7x, 256 devices: a whole 4x4x8 slice. The times are simulated.
256 devices in a mesh: ctx: 64 (over z, x, y_lo), dp: 4 (over y_hi, core).
Axes of the slice: x: 4, y: 4 (y_hi: 2, y_lo: 2; y = y_hi * 2 + y_lo), z: 8, core: 2. Of those that a mesh axis runs over, the one named last changes fastest.
Arguments:
- queries: bfloat16 [8192, 4096], P('ctx', 'dp'), may hold values from -100 to 100
- keys: bfloat16 [8192, 512], P('ctx', 'dp'), may hold values from -15 to 15
- values: bfloat16 [8192, 512], P('ctx', 'dp'), may hold values from -6 to 6
- segment_ids: int32 [8192], P('ctx'), may hold values from 0 to 3, never falling along the last dimension, each value on 1 to 4096 neighbouring positions
- cart_keys: bfloat16 [1024, 512], P('ctx', 'dp'), may hold values from -12 to 12
- cart_values: bfloat16 [1024, 512], P('ctx', 'dp'), may hold values from -6 to 6
Outputs:
- teacher_out: bfloat16 [8192, 4096], P('ctx', 'dp')
- student_out: bfloat16 [8192, 4096], P('ctx', 'dp')
- grad_keys: float32 [1024, 512], P('ctx')
- grad_values: float32 [1024, 512], P('ctx')
Inputs may be any that keep to these rules, and one draw needn't show every extreme that they name: `segment_ids`: document numbers never fall along the context; each document spans 1 to 4096 positions, one exactly that many.
All inputs are finite; a program needn't handle non-finite values.
Results may differ from a plain program's by a relative error of at most 0.0085.
The roundings to bfloat16 on the way count: a program that leaves them out, or rounds other values in their place, can miss the bound.
Values may be sent and summed in bfloat16 or wider, within the bound.
A program may use at most 64 MiB of HBM per device.

v0:
```python
import math

import jax
import jax.numpy as jnp
from jax import lax
from jax.sharding import PartitionSpec as P

HQ = 32
KVH = 4
HD = 128


distill_weight = 8.0
masked_score = -1e30


def per_device(queries, keys, values, segment_ids, cart_keys, cart_values):
    row_count = queries.shape[0]
    query_width = queries.shape[1]
    kv_local = keys.shape[1] // HD
    group_size = HQ // KVH
    score_scale = 1.0 / math.sqrt(HD)
    position = lax.axis_index("ctx")
    first_row = position * row_count
    last_row = first_row + row_count - 1
    query_heads = queries.reshape(row_count, kv_local, group_size, HD)
    query_pos = first_row + jnp.arange(row_count, dtype=jnp.int32)
    query_seg = segment_ids.astype(jnp.bfloat16)

    def attend(state, key_start, key_block, value_block, seg_block):
        running_max, running_sum, running_out = state
        width = key_block.shape[0]
        key_heads = key_block.reshape(width, kv_local, HD)
        value_heads = value_block.reshape(width, kv_local, HD)
        scores = (
            jnp.einsum("ikgd,jkd->kgij", query_heads, key_heads, preferred_element_type=jnp.float32)
            * score_scale
        )
        key_pos = key_start + jnp.arange(width, dtype=jnp.int32)
        allowed = (key_pos[None, :] <= query_pos[:, None]) & (
            seg_block[None, :] == query_seg[:, None]
        )
        scores = jnp.where(allowed[None, None], scores, masked_score)
        new_max = jnp.maximum(running_max, jnp.max(scores, axis=-1))
        factor = jnp.exp(running_max - new_max)
        weights = jnp.exp(scores - new_max[..., None])
        running_sum = running_sum * factor + jnp.sum(weights, axis=-1)
        running_out = running_out * factor[..., None] + jnp.einsum(
            "kgij,jkd->kgid",
            weights.astype(jnp.bfloat16),
            value_heads,
            preferred_element_type=jnp.float32,
        )
        return (new_max, running_sum, running_out)

    state = (
        jnp.full((kv_local, group_size, row_count), masked_score, jnp.float32),
        jnp.zeros((kv_local, group_size, row_count), jnp.float32),
        jnp.zeros((kv_local, group_size, row_count, HD), jnp.float32),
    )
    current = state
    key_piece = lax.all_gather(keys, "ctx", axis=0, tiled=True)
    value_piece = lax.all_gather(values, "ctx", axis=0, tiled=True)
    seg_piece = lax.all_gather(query_seg, "ctx", axis=0, tiled=True)
    width = min(row_count, key_piece.shape[0])
    count = key_piece.shape[0] // width

    def visit(inner, inputs):
        index, key_block, value_block, seg_block = inputs
        key_start = index * width
        inner = lax.cond(
            key_start <= last_row,
            lambda held: attend(held, key_start, key_block, value_block, seg_block),
            lambda held: held,
            inner,
        )
        return (inner, None)

    current, unused = lax.scan(
        visit,
        current,
        (
            jnp.arange(count, dtype=jnp.int32),
            key_piece.reshape(count, width, key_piece.shape[1]),
            value_piece.reshape(count, width, value_piece.shape[1]),
            seg_piece.reshape(count, width),
        ),
    )
    state = current
    running_max, running_sum, running_out = state
    teacher_heads = running_out / running_sum[..., None]
    teacher_rows = (
        jnp.transpose(teacher_heads, (2, 0, 1, 3))
        .reshape(row_count, query_width)
        .astype(jnp.bfloat16)
    )
    slot_keys, slot_values = (
        lax.all_gather(cart_keys, "ctx", axis=0, tiled=True),
        lax.all_gather(cart_values, "ctx", axis=0, tiled=True),
    )
    slot_count = slot_keys.shape[0]
    slot_key_heads = slot_keys.reshape(slot_count, kv_local, HD)
    slot_value_heads = slot_values.reshape(slot_count, kv_local, HD)
    target = teacher_rows.reshape(row_count, kv_local, group_size, HD)
    head_query = query_heads[:, 0]
    head_keys = slot_key_heads[:, 0]
    head_values = slot_value_heads[:, 0]
    logits = (
        jnp.einsum("igd,sd->gis", head_query, head_keys, preferred_element_type=jnp.float32)
        * score_scale
    )
    probs = jax.nn.softmax(logits, axis=-1)
    probs_low = probs.astype(jnp.bfloat16)
    student = jnp.einsum("gis,sd->igd", probs_low, head_values, preferred_element_type=jnp.float32)
    delta = (distill_weight * (student - target[:, 0].astype(jnp.float32))).astype(jnp.bfloat16)
    back = jnp.einsum("igd,sd->gis", delta, head_values, preferred_element_type=jnp.float32)
    row_term = jnp.einsum("igd,igd->gi", delta.astype(jnp.float32), student)
    score_grad = (probs * (back - row_term[..., None])).astype(jnp.bfloat16)
    value_grads = [jnp.einsum("gis,igd->sd", probs_low, delta, preferred_element_type=jnp.float32)]
    key_grads = [
        jnp.einsum("gis,igd->sd", score_grad, head_query, preferred_element_type=jnp.float32)
        * score_scale
    ]
    student_list = [student.astype(jnp.bfloat16)]
    student_rows = jnp.stack(student_list, axis=1).reshape(row_count, query_width)
    relaid = lax.all_to_all(student_rows, "ctx", split_axis=0, concat_axis=0, tiled=True)
    local_width = kv_local * HD
    grads = jnp.concatenate(
        [
            jnp.stack(key_grads, axis=1).reshape(slot_count, local_width),
            jnp.stack(value_grads, axis=1).reshape(slot_count, local_width),
        ],
        axis=1,
    )
    summed = lax.psum(grads, "ctx")
    share = slot_count // lax.axis_size("ctx")
    owned = lax.dynamic_slice_in_dim(summed, lax.axis_index("ctx") * share, share, 0)
    key_full, value_full = (
        lax.all_gather(owned[:, :local_width], "dp", axis=1, tiled=True),
        lax.all_gather(owned[:, local_width:], "dp", axis=1, tiled=True),
    )
    return (teacher_rows, relaid, key_full, value_full)


def solution(mesh):
    in_specs = (
        P("ctx", "dp"),
        P("ctx", "dp"),
        P("ctx", "dp"),
        P("ctx"),
        P("ctx", "dp"),
        P("ctx", "dp"),
    )
    out_specs = (P("ctx", "dp"), P("ctx", "dp"), P("ctx", None), P("ctx", None))
    return jax.shard_map(
        per_device, mesh=mesh, in_specs=in_specs, out_specs=out_specs, check_vma=False
    )
```

profile of v0, /device:TPU:1, one launch (start us, length us, event | category | flops | bytes accessed | tf_op | source)
XLA Modules:
  0.0 1500.4 jit_solution(12708167369714326601)
XLA Ops:
  7.2 0.7 all-gather.4.cloned.1.call-update
  7.9 0.7 all-gather.6.cloned.1.call-update
  8.7 0.7 fusion.54
  9.4 132.1 %all-gather = bf16[64,1,128]{2,1,0:T(2,128)(2,1)S(1)} all-gather(bf16[1,1,128]{2,1,0:T(2,128)(2,1)S(1)} %get-tuple-element.277), channel_id=1, replica_groups=mesh['ctx'=64,'dp'=4] {'ctx'}, dimensions={0}, use_global_device_ids=true | all-gather | bytes 16640 | tf_op jit(solution)/shard_map/all_gather | solution.py:64
  141.5 1.1 copy.34
  142.8 126.1 %all_gather.25 = bf16[1024,128]{1,0:T(8,128)(2,1)S(1)} all-gather(bf16[16,128]{1,0:T(8,128)(2,1)} %param.15), channel_id=1, replica_groups=mesh['ctx'=64,'dp'=4] {'ctx'}, dimensions={0}, use_global_device_ids=true | all-gather | bytes 266240 | tf_op jit(solution)/shard_map/all_gather | solution.py:99
  268.8 126.9 %all_gather.24 = bf16[1024,128]{1,0:T(8,128)(2,1)S(1)} all-gather(bf16[16,128]{1,0:T(8,128)(2,1)} %param.14), channel_id=1, replica_groups=mesh['ctx'=64,'dp'=4] {'ctx'}, dimensions={0}, use_global_device_ids=true | all-gather | bytes 266240 | tf_op jit(solution)/shard_map/all_gather | solution.py:98
  395.7 3.3 fusion.55
  399.0 2.5 fusion.28
  401.6 163.9 %all-gather.6.cloned.1.call-done = bf16[8192,128]{1,0:T(8,128)(2,1)} async-done(((bf16[128,128]{1,0:T(8,128)(2,1)}), bf16[8192,128]{1,0:T(8,128)(2,1)}) %all-gather.6.cloned.1.call-update) | async-done | bytes 2097168 | tf_op jit(solution)/shard_map/all_gather | solution.py:63
  565.6 91.0 %while.15 = (s32[]{:T(128)}, f32[1,8,128]{2,1,0:T(8,128)S(1)}, f32[1,8,128]{2,1,0:T(8,128)S(1)}, f32[1,8,128,128]{3,2,1,0:T(8,128)S(1)}, s32[64]{0:T(128)S(1)}, ...) while((s32[]{:T(128)}, f32[1,8,128]{2,1,0:T(8,128)S(1)}, ...), condition=%wide.region_5.6_spmd.clone, body=%wide.region_0.5_spmd.clone.sunk | while | flops 68373760 | bytes 3052887 | solution.py:79
  565.6 0.6 dynamic_slice.51
  567.0 2.5 conditional.3
  567.1 1.0 fusion.52
  568.2 1.2 fusion.3
  569.5 0.6 dynamic_slice.51
  570.9 0.6 dynamic_slice.51
  572.3 0.6 dynamic_slice.51
  573.6 0.6 dynamic_slice.51
  575.0 0.6 dynamic_slice.51
  580.6 0.6 dynamic_slice.51
  581.9 0.6 dynamic_slice.51
  583.3 0.6 dynamic_slice.51
  584.7 0.6 dynamic_slice.51
  586.1 0.6 dynamic_slice.51
  587.5 0.6 dynamic_slice.51
  593.0 0.6 dynamic_slice.51
  594.4 0.6 dynamic_slice.51
  595.8 0.6 dynamic_slice.51
  597.2 0.6 dynamic_slice.51
  598.5 0.6 dynamic_slice.51
  599.9 0.6 dynamic_slice.51
  601.3 0.6 dynamic_slice.51
  606.8 0.6 dynamic_slice.51
  608.2 0.6 dynamic_slice.51
  609.6 0.6 dynamic_slice.51
  611.0 0.6 dynamic_slice.51
  612.4 0.6 dynamic_slice.51
  613.8 0.6 dynamic_slice.51
  619.3 0.6 dynamic_slice.51
  620.7 0.6 dynamic_slice.51
  622.1 0.6 dynamic_slice.51
  623.4 0.6 dynamic_slice.51
  624.8 0.6 dynamic_slice.51
  626.2 0.6 dynamic_slice.51
  627.6 0.6 dynamic_slice.51
  633.1 0.6 dynamic_slice.51
  634.5 0.6 dynamic_slice.51
  635.9 0.6 dynamic_slice.51
  656.6 1.6 fusion.34
  658.2 0.8 convolution_bitcast_fusion.1
  659.0 3.7 fusion.31
  662.8 1.1 pad_maximum_fusion
  664.1 0.8 all_to_all.8
  664.9 162.9 %all-to-all-start = ((bf16[64,2,1024]{2,1,0:T(2,128)(2,1)}), bf16[64,2,1024]{2,1,0:T(2,128)(2,1)S(1)}, u32[]{:S(2)}, u32[]{:S(2)}) async-start(bf16[64,2,1024]{2,1,0:T(2,128)(2,1)} %all_to_all.8), calls=%async_computation | async-start | bytes 524288 | tf_op jit(solution)/shard_map/all_to_all | solution.py:126
  828.0 0.9 copy.45
  828.8 9.6 all-to-all-done
  838.4 0.8 all_to_all.10
  839.2 593.9 %all-reduce.2.cloned.1.call-done = f32[1024,256]{0,1:T(8,128)} async-done(((f32[1024,256]{0,1:T(8,128)}), f32[1024,256]{0,1:T(8,128)}) %all-reduce.2.cloned.1.call-update) | async-done | bytes 1048592 | tf_op jit(solution)/shard_map/psum | solution.py:135
  1433.1 1.0 fusion.53
  1434.0 51.0 %all_gather.27 = f32[16,512]{0,1:T(8,128)S(1)} all-gather(f32[16,128]{0,1:T(8,128)S(1)} %get-tuple-element.273), channel_id=1, replica_groups=mesh['ctx'=64,'dp'=4] {'dp'}, dimensions={1}, use_global_device_ids=true | all-gather | bytes 40960 | tf_op jit(solution)/shard_map/all_gather | solution.py:140
  1485.1 0.7 copy.47
  1485.8 7.3 all_gather.26
  1493.1 0.7 copy.46
  (180 shorter events, 20.8 us)
Async XLA Ops:
  7.2 394.5 %all-gather.4.cloned.1.call-start = ((), (), s32[]{:S(2)}) async-start(), calls=%async_computation.1 | async-start | bytes 2129920 | tf_op jit(solution)/shard_map/all_gather | solution.py:62
  7.9 557.7 %all-gather.6.cloned.1.call-start = ((), (), s32[]{:S(2)}) async-start(), calls=%async_computation.2 | async-start | bytes 2129920 | tf_op jit(solution)/shard_map/all_gather | solution.py:63
  8.6 1424.4 %all-reduce.2.cloned.1.call-start = ((), (), s32[]{:S(2)}) async-start(), calls=%async_computation.3 | async-start | bytes 2097152 | tf_op jit(solution)/shard_map/psum | solution.py:135
  658.2 0.8 copy-start
  659.0 4.9 copy-start.1
  664.9 173.5 %all-to-all-start = ((bf16[64,2,1024]{2,1,0:T(2,128)(2,1)}), bf16[64,2,1024]{2,1,0:T(2,128)(2,1)S(1)}, u32[]{:S(2)}, u32[]{:S(2)}) async-start(bf16[64,2,1024]{2,1,0:T(2,128)(2,1)} %all_to_all.8), calls=%async_computation | async-start | bytes 524288 | tf_op jit(solution)/shard_map/all_to_all | solution.py:126
Sparse Core Ops, SparseCore 0:
  9.8 256.8 all-gather.3
  268.4 297.0 all-gather.5
  664.1 768.9 all-reduce.1
where the time goes:
time: 1510 us; the launch traced here: 1500 us
  waiting for transfers between devices  769 us (51%)
  blocking collectives  443 us (29%)
  starting transfers between devices  163 us (11%)
  local copies, waits for them, and re-layouts  48.3 us (3%)
  loops' own time  46.9 us (3%)
    psum x1, waiting for transfers between devices, per_device(): summed = lax.psum(grads, 'ctx')  594 us
    all_gather x1, waiting for transfers between devices, per_device(): value_piece = lax.all_gather(values, 'ctx', axis=0, tiled=True)  164 us
    all_to_all x1, starting transfers between devices, per_device(): lax.all_to_all(student_rows, 'ctx', split_axis=0, concat_axis=0, tiled=True)  163 us
    all_gather x1, blocking collectives, per_device(): seg_piece = lax.all_gather(query_seg, 'ctx', axis=0, tiled=True)  132 us
    all_gather x1, blocking collectives, per_device(): lax.all_gather(cart_keys, 'ctx', axis=0, tiled=True)  127 us
    all_gather x1, blocking collectives, per_device(): lax.all_gather(cart_values, 'ctx', axis=0, tiled=True)  126 us
    all_gather x1, blocking collectives, per_device(): lax.all_gather(owned[:, local_width:], 'dp', axis=1, tiled=True)  51 us
    another operation x1, loops' own time, per_device(): lax.scan(visit, current, (jnp.arange(count, dtype=jnp.int32), key_piece.r...  45.9 us
  transfers between devices with their start and end apart: 4, of which 3 were waited for; matrix products, arithmetic and copies ran while one was open for 1% of the time, Pallas kernels for 0%

commit v1 on v0

v1 whole, which is shorter than its diff:
```python
import functools
import math

import jax
import jax.numpy as jnp
from jax import lax
from jax.experimental import pallas as pl
from jax.experimental.pallas import tpu as pltpu
from jax.sharding import PartitionSpec as P

HQ = 32
KVH = 4
HD = 128
NX, NY, NQ = 4, 2, 8
ROWS = 128
PAIRS = 4
WIDE = 256
F32, BF16 = jnp.float32, jnp.bfloat16
MESH = pl.DeviceIdType.MESH
MASKED = -1e30
WEIGHT = 8.0
SCALE = 1.0 / math.sqrt(HD)
EXP2_SCALE = SCALE * math.log2(math.e)


def dot_nn(a, b):
    return lax.dot_general(a, b, (((1,), (0,)), ((), ())), preferred_element_type=F32)


def dot_nt(a, b):
    return lax.dot_general(a, b, (((1,), (1,)), ((), ())), preferred_element_type=F32)


def kernel(
    NZ, NDP,
    q_ref, k_hbm, v_hbm, cart_hbm,
    t_out, s_out, gk_out, gv_out,
    kvbuf, cartbuf, qrows, vt, ck, cv, cvt, m_ref, l_ref, acc, p_ref, plow, ot_ref,
    sbuf, rbuf1, s2buf, rbuf2, gk_acc, gv_acc, gbuf, rs1, zbuf, rs2, fbuf, dbuf,
    loc_sem, send_sem, kvz_sem, kv_sem, cart_sem, cartz_sem, a1_sem, a2_sem, r1_sem, r2_sem, dp_sem,
):
    NP = min(5, NZ)
    me = lax.axis_index("ctx")
    d = lax.axis_index("dp")
    rem, div = lax.rem, lax.div
    z = div(me, NQ)
    q = rem(me, NQ)
    x = div(q, NY)
    y = rem(q, NY)
    xp, xm, xo, yo = rem(x + 1, NX), rem(x + 3, NX), rem(x + 2, NX), 1 - y
    zp, zm = rem(z + 1, NZ), rem(z + NZ - 1, NZ)

    def ctx(zz, qq):
        return zz * NQ + qq

    to_zp, to_zm = ctx(zp, q), ctx(zm, q)

    def qi(xx, yy):
        return xx * NY + yy

    sent = []

    def copy(src, dst, ssem, rsem, to, to_dp):
        return pltpu.make_async_remote_copy(
            src_ref=src, dst_ref=dst, send_sem=ssem, recv_sem=rsem,
            device_id=(to, to_dp), device_id_type=MESH,
        )

    def send(refs, to, to_dp=None, cond=None):
        slot = len(sent)

        def make():
            src, dst, rsem = refs()
            return copy(src, dst, send_sem.at[slot], rsem, to, d if to_dp is None else to_dp)

        sent.append((cond, make))
        make().start()

    def recv(dst, rsem):
        copy(dst, dst, send_sem.at[0], rsem, me, d).wait_recv()

    barrier = pltpu.get_barrier_semaphore()
    peers = 0
    for r in range(1, NQ):
        pl.semaphore_signal(barrier, 1, device_id=(ctx(z, rem(q + r, NQ)), d), device_id_type=MESH)
        peers += 1
    for r in range(1, NZ):
        pl.semaphore_signal(barrier, 1, device_id=(ctx(rem(z + r, NZ), q), d), device_id_type=MESH)
        peers += 1
    for r in range(1, NDP):
        pl.semaphore_signal(barrier, 1, device_id=(me, rem(d + r, NDP)), device_id_type=MESH)
        peers += 1

    own = [
        pltpu.make_async_copy(cart_hbm, cartbuf.at[z, q], loc_sem.at[0]),
        pltpu.make_async_copy(k_hbm, kvbuf.at[0, q, 0], loc_sem.at[1]),
        pltpu.make_async_copy(v_hbm, kvbuf.at[0, q, 1], loc_sem.at[2]),
    ]
    for c in own:
        c.start()
    for c in own:
        c.wait()
    pl.semaphore_wait(barrier, peers)

    def cart_start():
        for r in range(1, NQ):
            send(lambda: (cartbuf.at[z, q], cartbuf.at[z, q], cart_sem.at[q]), ctx(z, rem(q + r, NQ)))

    UP, DOWN = NZ // 2, NZ - 1 - NZ // 2

    def cart_hop(h):
        if h == 0:
            for r in range(1, NQ):
                s = rem(q + r, NQ)
                recv(cartbuf.at[z, s], cart_sem.at[s])
        elif h <= UP:
            s = rem(z + NZ - h, NZ)
            recv(cartbuf.at[s], cartz_sem.at[s])
        if h < UP:
            s = rem(z + NZ - h, NZ)
            send(lambda s=s: (cartbuf.at[s], cartbuf.at[s], cartz_sem.at[s]), to_zp)
        if 1 <= h <= DOWN:
            s = rem(z + h, NZ)
            recv(cartbuf.at[s], cartz_sem.at[s])
        if h < DOWN:
            s = rem(z + h, NZ)
            send(lambda s=s: (cartbuf.at[s], cartbuf.at[s], cartz_sem.at[s]), to_zm)

    def when(k, body):
        if k == 0:
            body(None)
        else:
            pl.when(z >= k)(lambda: body(k))

    def unit(k, qq, j):
        return kvbuf.at[k, qq, j]

    def half(k, qq, j, h):
        return kvbuf.at[k, qq, j, pl.ds(h * 64, 64)]

    def pass_on(k, cond, qq, j, to, h=None):
        if h is None:
            send(lambda: (unit(k, qq, j), unit(k, qq, j), kv_sem.at[k, qq, j, 0]), to, cond=cond)
        else:
            send(lambda: (half(k, qq, j, h), half(k, qq, j, h), kv_sem.at[k, qq, j, h]), to, cond=cond)

    def got(k, qq, j, h=None):
        if h is None:
            recv(unit(k, qq, j), kv_sem.at[k, qq, j, 0])
        else:
            recv(half(k, qq, j, h), kv_sem.at[k, qq, j, h])

    at = {(n, m): qi(xx, yy) for n, xx in (("0", x), ("-", xm), ("+", xp), ("o", xo)) for m, yy in ((0, y), (1, yo))}
    to_xp, to_xm, to_y = ctx(z, qi(xp, y)), ctx(z, qi(xm, y)), ctx(z, qi(x, yo))

    def z_step(k):
        if k > 0:
            @pl.when(z >= k)
            def _():
                recv(kvbuf.at[k, q], kvz_sem.at[k])
        if k + 1 < NP:
            slot_cond = ("z", k)
            @pl.when((z >= k) & (z < NZ - 1))
            def _():
                send(lambda: (kvbuf.at[k, q], kvbuf.at[k + 1, q], kvz_sem.at[k + 1]), to_zp, cond=slot_cond)

    def round0(k):
        def body(c):
            pass_on(k, c, q, 0, to_y)
            pass_on(k, c, q, 1, to_xp)
            pass_on(k, c, q, 1, to_xm)
            pass_on(k, c, q, 0, to_xp)
            pass_on(k, c, q, 0, to_xm)
            pass_on(k, c, q, 1, to_y)
        when(k, body)

    def round1(k):
        def body(c):
            s = at["0", 1]
            got(k, s, 0)
            pass_on(k, c, s, 0, to_xp)
            pass_on(k, c, s, 0, to_xm)
            sm, sp = at["-", 0], at["+", 0]
            got(k, sm, 1)
            pass_on(k, c, sm, 1, to_xp, 0)
            pass_on(k, c, sm, 1, to_y)
            got(k, sp, 1)
            pass_on(k, c, sp, 1, to_xm, 1)
            pass_on(k, c, sp, 1, to_y)
            got(k, sm, 0)
            pass_on(k, c, sm, 0, to_xp, 0)
            got(k, sp, 0)
            pass_on(k, c, sp, 0, to_xm, 1)
        when(k, body)

    def round2(k):
        def body(c):
            so = at["o", 0]
            got(k, so, 1, 0)
            got(k, so, 1, 1)
            pass_on(k, c, so, 1, to_y)
            sm, sp = at["-", 1], at["+", 1]
            got(k, sm, 0)
            pass_on(k, c, sm, 0, to_xp, 0)
            got(k, sp, 0)
            pass_on(k, c, sp, 0, to_xm, 1)
        when(k, body)

    def round3(k):
        def body(c):
            for m in (0, 1):
                got(k, at["o", m], 0, 0)
                got(k, at["o", m], 0, 1)
            for n in ("0", "-", "+", "o"):
                got(k, at[n, 1], 1)
        when(k, body)

    eye = (
        lax.broadcasted_iota(jnp.int32, (ROWS, ROWS), 0)
        == lax.broadcasted_iota(jnp.int32, (ROWS, ROWS), 1)
    ).astype(F32).astype(BF16)

    def swap_matrix():
        i = lax.broadcasted_iota(jnp.int32, (ROWS, ROWS), 0)
        j = lax.broadcasted_iota(jnp.int32, (ROWS, ROWS), 1)
        src = ((i >> 1) & 7) * 16 + (i >> 4) * 2 + (i & 1)
        return (src == j).astype(F32).astype(BF16)

    def prepare():
        for h in range(8):
            qrows[h * ROWS:(h + 1) * ROWS, :] = q_ref[:, h * HD:(h + 1) * HD]

    def teacher(k):
        def body(c):
            zk = rem(z + NZ - k, NZ)
            segs = cartbuf[zk, :, 32:48, :].astype(F32)
            own_seg = cartbuf[z, q, 32:48, :].astype(F32)[0:1, :]
            first = jnp.zeros((1, ROWS), F32)
            for s in (1, 2, 3):
                below = jnp.where(segs < s, 1.0, 0.0)
                below = jnp.sum(below, axis=0)
                below = jnp.sum(below, axis=0, keepdims=True)
                below = jnp.sum(below, axis=1, keepdims=True)
                first = jnp.where(own_seg == s, below, first)
            first = first.astype(jnp.int32)
            first = jnp.concatenate([first, first], axis=1)
            key_rows = kvbuf[k, :, 0].reshape(NQ * ROWS, HD)
            value_rows = kvbuf[k, :, 1].reshape(NQ * ROWS, HD)
            vt[...] = dot_nt(eye, value_rows).astype(BF16)
            last = q * ROWS + lax.broadcasted_iota(jnp.int32, (1, ROWS), 1)
            last = jnp.concatenate([last, last], axis=1)

            def pair(hp, carry):
                heads = qrows[pl.ds(pl.multiple_of(hp * WIDE, WIDE), WIDE), :]
                scores = dot_nt(key_rows, heads)
                pos = lax.broadcasted_iota(jnp.int32, scores.shape, 0)
                allowed = pos >= first
                if k == 0:
                    allowed = allowed & (pos <= last)
                scores = jnp.where(allowed, scores, MASKED)
                top = jnp.max(scores, axis=0, keepdims=True)
                if k > 0:
                    old = m_ref[hp]
                    top = jnp.maximum(top, old)
                    factor = jnp.exp2((old - top) * EXP2_SCALE)
                weights = jnp.exp2((scores - top) * EXP2_SCALE)
                total = jnp.sum(weights, axis=0, keepdims=True)
                mixed = dot_nn(vt[...], weights.astype(BF16))
                if k > 0:
                    total = total + l_ref[hp] * factor
                    mixed = mixed + acc[hp] * factor
                m_ref[hp] = top
                l_ref[hp] = total
                acc[hp] = mixed
                return carry

            lax.fori_loop(0, PAIRS, pair, 0)
        when(k, body)

    SL = NZ * NQ * 16

    def student():
        ck[...] = cartbuf[:, :, 0:16, :].reshape(SL, HD)
        cv[...] = cartbuf[:, :, 16:32, :].reshape(SL, HD)
        cvt[...] = dot_nt(eye, cv[...]).astype(BF16)
        swap = swap_matrix()

        for hp in range(PAIRS):
            heads = qrows[hp * WIDE:(hp + 1) * WIDE, :]
            logits = dot_nt(ck[...], heads)
            top = jnp.max(logits, axis=0, keepdims=True)
            expo = jnp.exp2((logits - top) * EXP2_SCALE)
            total = jnp.sum(expo, axis=0, keepdims=True)
            probs = expo * (1.0 / total)
            low = probs.astype(BF16)
            p_ref[hp] = probs
            plow[hp] = low
            out = dot_nn(cvt[...], low)
            ot_ref[hp] = out
            out_low = out.astype(BF16)
            for g in range(2):
                h = hp * 2 + g
                rows = dot_nt(swap, out_low[:, g * ROWS:(g + 1) * ROWS])
                sbuf[:, :, h * HD:(h + 1) * HD] = rows.astype(BF16).reshape(NQ, 16, HD)

    def exchange1():
        for r in range(1, NQ):
            t = rem(q + r, NQ)
            send(lambda t=t: (sbuf.at[t], rbuf1.at[q], a1_sem.at[q]), ctx(z, t))

    def exchange2():
        for r in range(1, NQ):
            s = rem(q + r, NQ)
            recv(rbuf1.at[s], a1_sem.at[s])
        rbuf1[q] = sbuf[q]
        swap = swap_matrix()
        s2buf[...] = dot_nn(swap, rbuf1[...].reshape(ROWS, 1024)).astype(BF16).reshape(NQ, 16, 1024)
        for r in range(1, NZ):
            t = rem(z + r, NZ)
            send(lambda t=t: (s2buf.at[t], rbuf2.at[z], a2_sem.at[z]), ctx(t, q))

    def exchange3():
        for r in range(1, NZ):
            s = rem(z + r, NZ)
            recv(rbuf2.at[s], a2_sem.at[s])
        rbuf2[z] = s2buf[z]
        s_out[...] = rbuf2[...].reshape(NZ * 16, 1024)

    def backward():
        for hp in range(PAIRS):
            low_t = (acc[hp] / l_ref[hp]).astype(BF16)
            out = ot_ref[hp]
            delta = (WEIGHT * (out - low_t.astype(F32))).astype(BF16)
            for g in range(2):
                h = hp * 2 + g
                t_out[:, h * HD:(h + 1) * HD] = dot_nt(eye, low_t[:, g * ROWS:(g + 1) * ROWS]).astype(BF16)
            row_term = jnp.sum(delta.astype(F32) * out, axis=0, keepdims=True)
            back = dot_nn(cv[...], delta)
            ds = (p_ref[hp] * (back - row_term)).astype(BF16)
            gv = dot_nt(plow[hp], delta)
            gk = dot_nn(ds, qrows[hp * WIDE:(hp + 1) * WIDE, :])
            if hp > 0:
                gv = gv + gv_acc[...]
                gk = gk + gk_acc[...]
            if hp < PAIRS - 1:
                gv_acc[...] = gv
                gk_acc[...] = gk
            else:
                gbuf[:, :, 0] = (gk * SCALE).astype(BF16).reshape(NZ, NQ, 16, HD)
                gbuf[:, :, 1] = gv.astype(BF16).reshape(NZ, NQ, 16, HD)

    def reduce1():
        for r in range(1, NQ):
            t = rem(q + r, NQ)
            send(lambda t=t: (gbuf.at[:, t], rs1.at[q], r1_sem.at[q]), ctx(z, t))

    def reduce2():
        total = gbuf[:, q].astype(F32)
        for r in range(1, NQ):
            s = rem(q + r, NQ)
            recv(rs1.at[s], r1_sem.at[s])
            total = total + rs1[s].astype(F32)
        zbuf[...] = total.astype(BF16)
        for r in range(1, NZ):
            t = rem(z + r, NZ)
            send(lambda t=t: (zbuf.at[t], rs2.at[z], r2_sem.at[z]), ctx(t, q))

    def reduce3():
        total = zbuf[z].astype(F32)
        for r in range(1, NZ):
            s = rem(z + r, NZ)
            recv(rs2.at[s], r2_sem.at[s])
            total = total + rs2[s].astype(F32)
        fbuf[...] = total
        for r in range(1, NDP):
            t = rem(d + r, NDP)
            send(lambda: (fbuf, dbuf.at[d], dp_sem.at[d]), me, to_dp=t)
        dbuf[d] = total

    def reduce4():
        for r in range(1, NDP):
            s = rem(d + r, NDP)
            recv(dbuf.at[s], dp_sem.at[s])
        for s in range(NDP):
            gk_out[:, s * HD:(s + 1) * HD] = dbuf[s, 0]
            gv_out[:, s * HD:(s + 1) * HD] = dbuf[s, 1]

    cart_start()
    z_step(0)
    round0(0)
    prepare()
    STEPS = NP + 3
    hops = max(UP, DOWN) + 1
    fed = max(hops, 5)
    for t in range(1, max(STEPS, fed + 2)):
        if t - 1 < hops:
            cart_hop(t - 1)
        if t < NP:
            z_step(t)
        for age, part in ((2, round2), (1, round1), (0, round0)):
            if 0 <= t - age < NP:
                part(t - age)
        if t == fed:
            student()
            exchange1()
        if 0 <= t - 3 < NP:
            round3(t - 3)
            teacher(t - 3)
        if t == fed + 1:
            exchange2()
    backward()
    reduce1()
    exchange3()
    reduce2()
    reduce3()
    reduce4()
    for cond, make in sent:
        if cond is None:
            make().wait_send()
        elif isinstance(cond, tuple):
            pl.when((z >= cond[1]) & (z < NZ - 1))(lambda: make().wait_send())
        else:
            pl.when(z >= cond)(lambda: make().wait_send())


def per_device(NZ, NDP, queries, keys, values, segment_ids, cart_keys, cart_values):
    NP = min(5, NZ)
    SL = NZ * NQ * 16
    seg = jnp.broadcast_to(segment_ids.astype(BF16)[None, :], (16, ROWS))
    seg = jnp.where(jnp.arange(16)[:, None] == 0, seg, jnp.bfloat16(100.0))
    cart = jnp.concatenate([cart_keys, cart_values, seg], axis=0)
    V = pltpu.VMEM
    D = pltpu.SemaphoreType.DMA
    vmem = pl.BlockSpec(memory_space=pltpu.VMEM)
    hbm = pl.BlockSpec(memory_space=pl.ANY)
    return pl.pallas_call(
        functools.partial(kernel, NZ, NDP),
        out_shape=[
            jax.ShapeDtypeStruct((ROWS, 1024), BF16),
            jax.ShapeDtypeStruct((NZ * 16, 1024), BF16),
            jax.ShapeDtypeStruct((16, NDP * HD), F32),
            jax.ShapeDtypeStruct((16, NDP * HD), F32),
        ],
        in_specs=[vmem, hbm, hbm, hbm],
        out_specs=[vmem] * 4,
        scratch_shapes=[
            V((NP, NQ, 2, ROWS, HD), BF16),
            V((NZ, NQ, 48, HD), BF16),
            V((1024, HD), BF16),
            V((HD, NQ * ROWS), BF16),
            V((SL, HD), BF16),
            V((SL, HD), BF16),
            V((HD, SL), BF16),
            V((PAIRS, 1, WIDE), F32),
            V((PAIRS, 1, WIDE), F32),
            V((PAIRS, HD, WIDE), F32),
            V((PAIRS, SL, WIDE), F32),
            V((PAIRS, SL, WIDE), BF16),
            V((PAIRS, HD, WIDE), F32),
            V((NQ, 16, 1024), BF16),
            V((NQ, 16, 1024), BF16),
            V((NQ, 16, 1024), BF16),
            V((NZ, 16, 1024), BF16),
            V((SL, HD), F32),
            V((SL, HD), F32),
            V((NZ, NQ, 2, 16, HD), BF16),
            V((NQ, NZ, 2, 16, HD), BF16),
            V((NZ, 2, 16, HD), BF16),
            V((NZ, 2, 16, HD), BF16),
            V((2, 16, HD), F32),
            V((NDP, 2, 16, HD), F32),
            D((3,)), D((160,)), D((NP,)), D((NP, NQ, 2, 2)), D((NQ,)), D((NZ,)),
            D((NQ,)), D((NZ,)), D((NQ,)), D((NZ,)), D((NDP,)),
        ],
        compiler_params=pltpu.CompilerParams(
            collective_id=0, has_side_effects=True, vmem_limit_bytes=60 * 1024 * 1024
        ),
        name="distill",
    )(queries, keys, values, cart)


def solution(mesh):
    nz, ndp = mesh.shape["ctx"] // NQ, mesh.shape["dp"]
    specs = (
        P("ctx", "dp"), P("ctx", "dp"), P("ctx", "dp"), P("ctx"), P("ctx", "dp"), P("ctx", "dp"),
    )
    return jax.shard_map(
        functools.partial(per_device, nz, ndp), mesh=mesh, in_specs=specs,
        out_specs=(P("ctx", "dp"), P("ctx", "dp"), P("ctx", None), P("ctx", None)),
        check_vma=False,
    )
```

time: 1510 us -> 78.8 us (0.05)
  waiting for transfers between devices: 769 us -> 0 us
  blocking collectives: 443 us -> 0 us
  starting transfers between devices: 163 us -> 0 us
  Pallas kernels: 0 us -> 72.5 us
  loops' own time: 46.9 us -> 0 us
  local copies, waits for them, and re-layouts: 48.3 us -> 3.87 us
    psum x1 -> x0, waiting for transfers between devices: 594 us -> none  [per_device(): summed = lax.psum(grads, 'ctx')]
    all_gather x5 -> x0, blocking collectives: 443 us -> none  [the longest x1 132 us: per_device(): seg_piece = lax.all_gather(query_seg, 'ctx', axis=0, tiled=True)]
    all_gather x2 -> x0, waiting for transfers between devices: 164 us -> none  [the longest x1 164 us: per_device(): value_piece = lax.all_gather(values, 'ctx', axis=0, tiled=True)]
    all_to_all x1 -> x0, starting transfers between devices: 163 us -> none  [per_device(): lax.all_to_all(student_rows, 'ctx', split_axis=0, concat_axis=0, tiled=True)]
    pallas_call x0 -> x1, Pallas kernels: none -> 72.5 us  [per_device(): pl.pallas_call(functools.partial(kernel, NZ, NDP), out_shape=[jax.ShapeDt...]
    another operation x65 -> x0, loops' own time: 46.9 us -> none  [the longest x1 45.9 us: per_device(): lax.scan(visit, current, (jnp.arange(count, dtype=jnp.int32), key_piece.r...]
    dynamic_slice x65 -> x0, local copies, waits for them, and re-layouts: 41.6 us -> none  [per_device(): lax.scan(visit, current, (jnp.arange(count, dtype=jnp.int32), key_piece.r...]
  transfers between devices with their start and end apart: 4 -> 0, of which waited for: 3 -> 0; matrix products, arithmetic and copies ran while one was open for 1% -> 0% of each run, Pallas kernels for 0% -> 0%
where the time goes in v1:
time: 78.8 us; the launch traced here: 78.4 us
  Pallas kernels  72.5 us (92%)
  local copies, waits for them, and re-layouts  3.87 us (5%)
  other arithmetic  1.36 us (2%)
    pallas_call x1, Pallas kernels, per_device(): pl.pallas_call(functools.partial(kernel, NZ, NDP), out_shape=[jax.ShapeDt...  72.5 us
    unnamed x14, local copies, waits for them, and re-layouts  3.87 us

profile of v1, /device:TPU:1, one launch (start us, length us, event | category | flops | bytes accessed | tf_op | source)
XLA Modules:
  0.0 78.4 jit_solution(3544184170224896521)
XLA Ops:
  0.6 0.0 copy-start.3
  0.6 0.0 copy-start.4
  0.7 0.7 convert_element_type.3
  1.3 0.1 broadcast_select_fusion
  1.4 0.0 copy-done.3
  1.4 0.0 copy-done.4
  1.4 0.6 pad_maximum_fusion.cart_hbm
  2.0 72.5 %distill.1 = (bf16[128,1024]{1,0:T(8,128)(2,1)}, bf16[128,1024]{1,0:T(8,128)(2,1)}, f32[16,512]{1,0:T(8,128)}, f32[16,512]{1,0:T(8,128)}) custom-call(bf16[128,1024]{1,0:T(8,128)(2,1)} %q_ref.1, bf16[128,128]{1,0:T(8,128)(2,1)} %k_hbm.1, bf16[128,128]{1,0:T(8,128)(2,1)} %v_hbm.1, bf16[48,128]{1,0:T(8,128)(2,1)} %pad_maximum_fusion.cart_hbm), custom_call_target="tpu_custom_call" | custom-call | tf_op jit(solution)/shard_map/distill/pallas_call | solution.py:436
  74.6 0.0 copy-start
  74.6 1.7 %copy.14 = bf16[128,1024]{1,0:T(8,128)(2,1)} copy(bf16[128,1024]{1,0:T(8,128)(2,1)} %get-tuple-element.8) | data formatting | bytes 524288
  76.3 0.0 copy-done
  76.3 0.0 copy-start.2
  76.3 0.7 copy.15
  77.0 0.1 copy-done.2
  77.0 0.0 copy-start.1
  77.0 0.6 copy.16
  77.7 0.2 copy-done.1
  77.8 0.6 copy.17
  (1 shorter events, 0.0 us)
Async XLA Ops:
  0.6 0.8 copy-start.3
  0.6 0.8 copy-start.4
  74.6 1.7 %copy-start = (bf16[128,1024]{1,0:T(8,128)(2,1)S(1)}, bf16[128,1024]{1,0:T(8,128)(2,1)}, u32[]{:S(2)}) copy-start(bf16[128,1024]{1,0:T(8,128)(2,1)} %get-tuple-element.9) | copy-start | bytes 786436
  76.3 0.8 copy-start.2
  77.0 0.8 copy-start.1

commit v2 on v1

v2 whole, which is shorter than its diff:
```python
import functools
import math

import jax
import jax.numpy as jnp
from jax import lax
from jax.experimental import pallas as pl
from jax.experimental.pallas import tpu as pltpu
from jax.sharding import PartitionSpec as P

HQ = 32
KVH = 4
HD = 128
NX, NY, NQ = 4, 2, 8
ROWS = 128
PAIRS = 4
WIDE = 256
F32, BF16 = jnp.float32, jnp.bfloat16
MESH = pl.DeviceIdType.MESH
MASKED = -1e30
WEIGHT = 8.0
SCALE = 1.0 / math.sqrt(HD)
EXP2_SCALE = SCALE * math.log2(math.e)


def dot_nn(a, b):
    return lax.dot_general(a, b, (((1,), (0,)), ((), ())), preferred_element_type=F32)


def dot_nt(a, b):
    return lax.dot_general(a, b, (((1,), (1,)), ((), ())), preferred_element_type=F32)


def kernel(
    NZ, NDP,
    q_ref, k_hbm, v_hbm, seg_hbm, ck_hbm, cv_hbm,
    t_out, s_out, gk_out, gv_out,
    kvbuf, segbuf, cartbuf, qrows, vt, ck, cv, cvt, m_ref, l_ref, acc, p_ref, plow, ot_ref,
    delta_ref, row_ref, ds_ref,
    sbuf, rbuf1, s2buf, rbuf2, gbuf, rs1, zbuf, rs2, fbuf, dbuf,
    loc_sem, send_sem, kvz_sem, kv_sem, seg_sem, segz_sem, cart_sem, cartz_sem,
    a1_sem, a2_sem, r1_sem, r2_sem, dp_sem,
):
    NP = min(5, NZ)
    SL = NZ * NQ * 16
    rem, div = lax.rem, lax.div
    me = lax.axis_index("ctx")
    d = lax.axis_index("dp")
    z = div(me, NQ)
    q = rem(me, NQ)
    x = div(q, NY)
    y = rem(q, NY)

    def ctx(zz, qq):
        return rem(zz, NZ) * NQ + qq

    def at(dx, flip):
        return rem(x + dx, NX) * NY + (1 - y if flip else y)

    def guarded(cond, body):
        if cond is None:
            body()
        else:
            pl.when(cond())(body)

    sent = []

    def send(refs, to, cond=None):
        slot = len(sent)

        def make():
            src, dst, rsem = refs()
            place, part = to()
            return pltpu.make_async_remote_copy(
                src_ref=src, dst_ref=dst, send_sem=send_sem.at[slot], recv_sem=rsem,
                device_id=(place, part), device_id_type=MESH,
            )

        sent.append((cond, make))
        guarded(cond, lambda: make().start())

    def recv(refs, cond=None):
        def body():
            dst, rsem = refs()
            pltpu.make_async_remote_copy(
                src_ref=dst, dst_ref=dst, send_sem=send_sem.at[0], recv_sem=rsem,
                device_id=(me, d), device_id_type=MESH,
            ).wait_recv()

        guarded(cond, body)

    barrier = pltpu.get_barrier_semaphore()

    def greet():
        for r in range(1, NZ):
            pl.semaphore_signal(barrier, 1, device_id=(ctx(z + r, q), d), device_id_type=MESH)
        for r in range(1, NDP):
            pl.semaphore_signal(barrier, 1, device_id=(me, rem(d + r, NDP)), device_id_type=MESH)
        for r in range(1, NQ):
            pl.semaphore_signal(barrier, 1, device_id=(ctx(z, rem(q + r, NQ)), d), device_id_type=MESH)

    def own_copies():
        return [
            pltpu.make_async_copy(k_hbm, kvbuf.at[0, q, pl.ds(0, ROWS)], loc_sem.at[0]),
            pltpu.make_async_copy(v_hbm, kvbuf.at[0, q, pl.ds(ROWS, ROWS)], loc_sem.at[1]),
            pltpu.make_async_copy(seg_hbm, segbuf.at[0, q], loc_sem.at[2]),
            pltpu.make_async_copy(ck_hbm, cartbuf.at[z, q, 0], loc_sem.at[3]),
            pltpu.make_async_copy(cv_hbm, cartbuf.at[z, q, 1], loc_sem.at[4]),
        ]

    def seg_start():
        for r in range(1, NQ):
            send(lambda: (segbuf.at[0, q], segbuf.at[0, q], seg_sem.at[q]),
                 lambda r=r: (ctx(z, rem(q + r, NQ)), d))

    def seg_spread():
        for r in range(1, NQ):
            recv(lambda r=r: (segbuf.at[0, rem(q + r, NQ)], seg_sem.at[rem(q + r, NQ)]))
        for k in range(1, NP):
            send(lambda k=k: (segbuf.at[0], segbuf.at[k], segz_sem.at[k]),
                 lambda k=k: (ctx(z + k, q), d), lambda k=k: z + k < NZ)

    def seg_wait(k):
        if k > 0:
            recv(lambda: (segbuf.at[k], segz_sem.at[k]), lambda: z >= k)

    def plane(r):
        return rem(z + r + NZ, NZ)

    def cart_start():
        for r in range(1, NQ):
            send(lambda: (cartbuf.at[z, q], cartbuf.at[z, q], cart_sem.at[q]),
                 lambda r=r: (ctx(z, rem(q + r, NQ)), d))

    near = [r for r in ((1, -1, 2, -2) if NZ >= 8 else range(1, NZ))]

    def cart_spread():
        for r in range(1, NQ):
            recv(lambda r=r: (cartbuf.at[z, rem(q + r, NQ)], cart_sem.at[rem(q + r, NQ)]))
        for r in near:
            send(lambda: (cartbuf.at[z], cartbuf.at[z], cartz_sem.at[z, 0]),
                 lambda r=r: (ctx(z + r + NZ, q), d))

    def cart_relay():
        if NZ < 8:
            return
        for r in (-2, 2):
            part = 0 if r < 0 else 1
            step = 1 if r < 0 else -1
            recv(lambda r=r: (cartbuf.at[plane(r)], cartz_sem.at[plane(r), 0]))
            send(lambda r=r: (cartbuf.at[plane(r)], cartbuf.at[plane(r)], cartz_sem.at[plane(r), 0]),
                 lambda step=step: (ctx(z + step + NZ, q), d))
            send(lambda r=r, p=part: (cartbuf.at[plane(r), pl.ds(p * 4, 4)], cartbuf.at[plane(r), pl.ds(p * 4, 4)],
                                      cartz_sem.at[plane(r), p]),
                 lambda step=step: (ctx(z + 2 * step + NZ, q), d))

    def cart_wait():
        if NZ < 8:
            for r in near:
                recv(lambda r=r: (cartbuf.at[plane(-r)], cartz_sem.at[plane(-r), 0]))
            return
        for r in (-1, 1, -3, 3):
            recv(lambda r=r: (cartbuf.at[plane(r)], cartz_sem.at[plane(r), 0]))
        for p in (0, 1):
            recv(lambda p=p: (cartbuf.at[plane(4), pl.ds(p * 4, 4)], cartz_sem.at[plane(4), p]))

    CUT = 96
    LOW, HIGH = (0, CUT), (CUT, 2 * ROWS - CUT)

    def piece(k, qq, part):
        return kvbuf.at[k, qq, pl.ds(part[0], part[1])]

    def need(k, src, dst):
        if k == 0:
            return lambda: dst() > src()
        if k == 4:
            return lambda: (z >= 4) & (dst() < src())
        return lambda: z >= k

    def exists(k):
        return None if k == 0 else (lambda: z >= k)

    def hand(k, src, dst, part, cond):
        i = 0 if part is LOW else 1
        send(lambda: (piece(k, src(), part), piece(k, src(), part), kv_sem.at[k, src(), i]),
             lambda: (ctx(z, dst()), d), cond)

    def take(k, src, part, cond):
        i = 0 if part is LOW else 1
        recv(lambda: (piece(k, src(), part), kv_sem.at[k, src(), i]), cond)

    home = lambda: q
    twin = lambda: at(0, True)

    def z_send(k, steps):
        send(lambda: (kvbuf.at[k, q], kvbuf.at[k + steps, q], kvz_sem.at[k + steps]),
             lambda: (ctx(z + steps, q), d), lambda: (z >= k) & (z + steps < NZ))

    def z_recv(k):
        recv(lambda: (kvbuf.at[k, q], kvz_sem.at[k]), lambda: z >= k)
        if k == 2:
            for steps in (1, 2):
                if k + steps < NP:
                    z_send(k, steps)

    def round0(k):
        hand(k, home, twin, LOW, exists(k))
        for dx in (2, 1, 3):
            there = lambda dx=dx: at(dx, False)
            hand(k, home, there, HIGH, need(k, home, there))
        for dx in (2, 1, 3):
            there = lambda dx=dx: at(dx, False)
            hand(k, home, there, LOW, need(k, home, there))
        hand(k, home, twin, HIGH, need(k, home, twin))

    def round1(k):
        take(k, twin, LOW, exists(k))
        for dx in (2, 1, 3):
            there = lambda dx=dx: at(dx, False)
            hand(k, twin, there, LOW, need(k, twin, there))
        for dx in (1, 3, 2):
            source = lambda dx=dx: at(dx, False)
            take(k, source, HIGH, need(k, source, home))
            hand(k, source, twin, HIGH, need(k, source, twin))

    def round2(k):
        for dx in (1, 3, 2):
            for flip in (False, True):
                source = lambda dx=dx, flip=flip: at(dx, flip)
                take(k, source, LOW, need(k, source, home))
        for dx in (0, 1, 3, 2):
            source = lambda dx=dx: at(dx, True)
            take(k, source, HIGH, need(k, source, home))

    eye = (
        lax.broadcasted_iota(jnp.int32, (ROWS, ROWS), 0)
        == lax.broadcasted_iota(jnp.int32, (ROWS, ROWS), 1)
    ).astype(F32).astype(BF16)

    def swap_matrix():
        i = lax.broadcasted_iota(jnp.int32, (ROWS, ROWS), 0)
        j = lax.broadcasted_iota(jnp.int32, (ROWS, ROWS), 1)
        src = ((i >> 1) & 7) * 16 + (i >> 4) * 2 + (i & 1)
        return (src == j).astype(F32).astype(BF16)

    def prepare():
        for h in range(8):
            qrows[h * ROWS:(h + 1) * ROWS, :] = q_ref[:, h * HD:(h + 1) * HD]
        for s in range(NQ):
            @pl.when(s > q)
            def _():
                kvbuf[0, s, ROWS:2 * ROWS, :] = jnp.zeros((ROWS, HD), BF16)
            if NP == 5:
                @pl.when(s < q)
                def _():
                    kvbuf[4, s, ROWS:2 * ROWS, :] = jnp.zeros((ROWS, HD), BF16)

    def teacher(k, c0=0, count=NQ, cond=None):
        def body():
            segs = segbuf[k].reshape(NQ, ROWS)
            own_seg = segbuf[0, q]
            first = jnp.zeros((1, ROWS), F32)
            for s in (1, 2, 3):
                below = jnp.where(segs < s, 1.0, 0.0)
                below = jnp.sum(below, axis=0, keepdims=True)
                below = jnp.sum(below, axis=1, keepdims=True)
                first = jnp.where(own_seg == s, below, first)
            first = first.astype(jnp.int32) - c0 * ROWS
            first = jnp.concatenate([first, first], axis=1)
            key_rows = kvbuf[k, c0:c0 + count, 0:ROWS, :].reshape(count * ROWS, HD)
            value_rows = kvbuf[k, c0:c0 + count, ROWS:2 * ROWS, :].reshape(count * ROWS, HD)
            vt[:, :count * ROWS] = dot_nt(eye, value_rows).astype(BF16)
            last = (q - c0) * ROWS + lax.broadcasted_iota(jnp.int32, (1, ROWS), 1)
            last = jnp.concatenate([last, last], axis=1)
            opening = k == 0 and c0 == 0

            def pair(hp, carry):
                heads = qrows[pl.ds(pl.multiple_of(hp * WIDE, WIDE), WIDE), :]
                scores = dot_nt(key_rows, heads)
                pos = lax.broadcasted_iota(jnp.int32, scores.shape, 0)
                allowed = pos >= first
                if k == 0:
                    allowed = allowed & (pos <= last)
                scores = jnp.where(allowed, scores, MASKED)
                top = jnp.max(scores, axis=0, keepdims=True)
                if not opening:
                    old = m_ref[hp]
                    top = jnp.maximum(top, old)
                    factor = jnp.exp2((old - top) * EXP2_SCALE)
                weights = jnp.exp2((scores - top) * EXP2_SCALE)
                total = jnp.sum(weights, axis=0, keepdims=True)
                mixed = dot_nn(vt[:, :count * ROWS], weights.astype(BF16))
                if not opening:
                    total = total + l_ref[hp] * factor
                    mixed = mixed + acc[hp] * factor
                m_ref[hp] = top
                l_ref[hp] = total
                acc[hp] = mixed
                return carry

            lax.fori_loop(0, PAIRS, pair, 0)

        guarded(cond, body)

    def teach(k):
        seg_wait(k)
        if k == 0:
            teacher(0, 0, 4)
            teacher(0, 4, 4, lambda: q >= 4)
        elif k == 4:
            teacher(4, 4, 4, lambda: z >= 4)
            teacher(4, 0, 4, lambda: (z >= 4) & (q < 4))
        else:
            teacher(k, 0, NQ, lambda: z >= k)

    def student():
        ck[...] = cartbuf[:, :, 0].reshape(SL, HD)
        cv[...] = cartbuf[:, :, 1].reshape(SL, HD)
        cvt[...] = dot_nt(eye, cv[...]).astype(BF16)
        swap = swap_matrix()
        for hp in range(PAIRS):
            cols = slice(hp * WIDE, (hp + 1) * WIDE)
            logits = dot_nt(ck[...], qrows[cols, :])
            top = jnp.max(logits, axis=0, keepdims=True)
            expo = jnp.exp2((logits - top) * EXP2_SCALE)
            total = jnp.sum(expo, axis=0, keepdims=True)
            probs = expo * (1.0 / total)
            low = probs.astype(BF16)
            p_ref[:, cols] = probs
            plow[:, cols] = low
            out = dot_nn(cvt[...], low)
            ot_ref[:, cols] = out
            out_low = out.astype(BF16)
            for g in range(2):
                h = hp * 2 + g
                rows = dot_nt(swap, out_low[:, g * ROWS:(g + 1) * ROWS])
                sbuf[:, :, h * HD:(h + 1) * HD] = rows.astype(BF16).reshape(NQ, 16, HD)

    def exchange1():
        for r in range(1, NQ):
            send(lambda r=r: (sbuf.at[rem(q + r, NQ)], rbuf1.at[q], a1_sem.at[q]),
                 lambda r=r: (ctx(z, rem(q + r, NQ)), d))

    def exchange2():
        for r in range(1, NQ):
            recv(lambda r=r: (rbuf1.at[rem(q + r, NQ)], a1_sem.at[rem(q + r, NQ)]))
        rbuf1[q] = sbuf[q]
        swap = swap_matrix()
        s2buf[...] = dot_nn(swap, rbuf1[...].reshape(ROWS, 1024)).astype(BF16).reshape(NQ, 16, 1024)
        for r in range(1, NZ):
            send(lambda r=r: (s2buf.at[plane(r)], rbuf2.at[z], a2_sem.at[z]),
                 lambda r=r: (ctx(z + r, q), d))

    def exchange3():
        for r in range(1, NZ):
            recv(lambda r=r: (rbuf2.at[plane(r)], a2_sem.at[plane(r)]))
        rbuf2[z] = s2buf[z]
        s_out[...] = rbuf2[...].reshape(NZ * 16, 1024)

    def difference():
        for hp in range(PAIRS):
            cols = slice(hp * WIDE, (hp + 1) * WIDE)
            low_t = (acc[hp] / l_ref[hp]).astype(BF16)
            out = ot_ref[:, cols]
            delta = (WEIGHT * (out - low_t.astype(F32))).astype(BF16)
            delta_ref[:, cols] = delta
            row_ref[:, cols] = jnp.sum(delta.astype(F32) * out, axis=0, keepdims=True)
            for g in range(2):
                h = hp * 2 + g
                t_out[:, h * HD:(h + 1) * HD] = dot_nt(eye, low_t[:, g * ROWS:(g + 1) * ROWS]).astype(BF16)

    NH = 2
    HZ = NZ // NH

    def gradients(half):
        n = SL // NH
        rows = slice(half * n, (half + 1) * n)
        for hp in range(PAIRS):
            cols = slice(hp * WIDE, (hp + 1) * WIDE)
            back = dot_nn(cv[rows, :], delta_ref[:, cols])
            ds_ref[:, cols] = (p_ref[rows, cols] * (back - row_ref[:, cols])).astype(BF16)
        gv = dot_nt(plow[rows, :], delta_ref[...])
        gk = dot_nn(ds_ref[...], qrows[...])
        planes = slice(half * HZ, (half + 1) * HZ)
        gbuf[planes, :, 0] = (gk * SCALE).astype(BF16).reshape(HZ, NQ, 16, HD)
        gbuf[planes, :, 1] = gv.astype(BF16).reshape(HZ, NQ, 16, HD)

    def reduce1(half):
        planes = pl.ds(half * HZ, HZ)
        for r in range(1, NQ):
            send(lambda r=r: (gbuf.at[planes, rem(q + r, NQ)], rs1.at[q, planes], r1_sem.at[q, half]),
                 lambda r=r: (ctx(z, rem(q + r, NQ)), d))

    def reduce2(half):
        planes = pl.ds(half * HZ, HZ)
        total = gbuf[planes, q].astype(F32)
        for r in range(1, NQ):
            recv(lambda r=r: (rs1.at[rem(q + r, NQ), planes], r1_sem.at[rem(q + r, NQ), half]))
        for r in range(1, NQ):
            total = total + rs1[rem(q + r, NQ), planes].astype(F32)
        zbuf[planes] = total.astype(BF16)
        for t in range(half * HZ, (half + 1) * HZ):
            send(lambda t=t: (zbuf.at[t], rs2.at[z], r2_sem.at[z]),
                 lambda t=t: (ctx(t, q), d), lambda t=t: z != t)

    def reduce3():
        total = zbuf[z].astype(F32)
        for r in range(1, NZ):
            recv(lambda r=r: (rs2.at[plane(r)], r2_sem.at[plane(r)]))
        for r in range(1, NZ):
            total = total + rs2[plane(r)].astype(F32)
        fbuf[...] = total
        for r in range(1, NDP):
            send(lambda: (fbuf, dbuf.at[d], dp_sem.at[d]), lambda r=r: (me, rem(d + r, NDP)))
        dbuf[d] = total

    def reduce4():
        for r in range(1, NDP):
            recv(lambda r=r: (dbuf.at[rem(d + r, NDP)], dp_sem.at[rem(d + r, NDP)]))
        for s in range(NDP):
            gk_out[:, s * HD:(s + 1) * HD] = dbuf[s, 0]
            gv_out[:, s * HD:(s + 1) * HD] = dbuf[s, 1]

    def finish():
        for cond, make in sent:
            guarded(cond, lambda: make().wait_send())

    have = lambda k, part: part(k) if k < NP else None
    greet()
    own = own_copies()
    for c in own:
        c.start()
    prepare()
    for c in own:
        c.wait()
    pl.semaphore_wait(barrier, NQ - 1 + NZ - 1 + NDP - 1)
    z_send(0, 1)
    if NP > 2:
        z_send(0, 2)
    seg_start()
    cart_start()
    round0(0)
    seg_spread()
    cart_spread()
    have(1, z_recv)
    have(1, round0)
    round1(0)
    have(2, z_recv)
    have(2, round0)
    cart_relay()
    have(1, round1)
    have(3, z_recv)
    have(3, round0)
    round2(0)
    teach(0)
    have(2, round1)
    have(4, z_recv)
    have(4, round0)
    have(1, round2)
    have(1, teach)
    have(3, round1)
    cart_wait()
    student()
    have(4, round1)
    exchange1()
    for k in (2, 3, 4):
        have(k, round2)
        have(k, teach)
    exchange2()
    difference()
    gradients(0)
    reduce1(0)
    gradients(1)
    reduce1(1)
    reduce2(0)
    reduce2(1)
    reduce3()
    exchange3()
    reduce4()
    finish()


def write_out(t_ref, s_ref, gk_ref, gv_ref, t_hbm, s_hbm, gk_hbm, gv_hbm, sem):
    pairs = ((t_ref, t_hbm), (s_ref, s_hbm), (gk_ref, gk_hbm), (gv_ref, gv_hbm))
    copies = [pltpu.make_async_copy(a, b, sem.at[i]) for i, (a, b) in enumerate(pairs)]
    for c in copies:
        c.start()
    for c in copies:
        c.wait()


def per_device(NZ, NDP, queries, keys, values, segment_ids, cart_keys, cart_values):
    NP = min(5, NZ)
    SL = NZ * NQ * 16
    V = pltpu.VMEM
    D = pltpu.SemaphoreType.DMA
    vmem = pl.BlockSpec(memory_space=pltpu.VMEM)
    hbm = pl.BlockSpec(memory_space=pl.ANY)
    shapes = [
        jax.ShapeDtypeStruct((ROWS, 1024), BF16),
        jax.ShapeDtypeStruct((NZ * 16, 1024), BF16),
        jax.ShapeDtypeStruct((16, NDP * HD), F32),
        jax.ShapeDtypeStruct((16, NDP * HD), F32),
    ]
    results = pl.pallas_call(
        functools.partial(kernel, NZ, NDP),
        out_shape=shapes,
        in_specs=[vmem, hbm, hbm, hbm, hbm, hbm],
        out_specs=[vmem] * 4,
        scratch_shapes=[
            V((NP, NQ, 2 * ROWS, HD), BF16),
            V((NP, NQ, 1, ROWS), jnp.int32),
            V((NZ, NQ, 2, 16, HD), BF16),
            V((1024, HD), BF16),
            V((HD, NQ * ROWS), BF16),
            V((SL, HD), BF16),
            V((SL, HD), BF16),
            V((HD, SL), BF16),
            V((PAIRS, 1, WIDE), F32),
            V((PAIRS, 1, WIDE), F32),
            V((PAIRS, HD, WIDE), F32),
            V((SL, 1024), F32),
            V((SL, 1024), BF16),
            V((HD, 1024), F32),
            V((HD, 1024), BF16),
            V((1, 1024), F32),
            V((SL // 2, 1024), BF16),
            V((NQ, 16, 1024), BF16),
            V((NQ, 16, 1024), BF16),
            V((NQ, 16, 1024), BF16),
            V((NZ, 16, 1024), BF16),
            V((NZ, NQ, 2, 16, HD), BF16),
            V((NQ, NZ, 2, 16, HD), BF16),
            V((NZ, 2, 16, HD), BF16),
            V((NZ, 2, 16, HD), BF16),
            V((2, 16, HD), F32),
            V((NDP, 2, 16, HD), F32),
            D((5,)), D((160,)), D((NP,)), D((NP, NQ, 2)), D((NQ,)), D((NP,)), D((NQ,)), D((NZ, 2)),
            D((NQ,)), D((NZ,)), D((NQ, 2)), D((NZ,)), D((NDP,)),
        ],
        compiler_params=pltpu.CompilerParams(
            collective_id=0, has_side_effects=True, vmem_limit_bytes=60 * 1024 * 1024
        ),
        name="distill",
    )(queries, keys, values, segment_ids.reshape(1, ROWS), cart_keys, cart_values)
    return pl.pallas_call(
        write_out, out_shape=shapes, in_specs=[vmem] * 4, out_specs=[hbm] * 4,
        scratch_shapes=[D((4,))], name="write_out",
    )(*results)


def solution(mesh):
    nz, ndp = mesh.shape["ctx"] // NQ, mesh.shape["dp"]
    specs = (
        P("ctx", "dp"), P("ctx", "dp"), P("ctx", "dp"), P("ctx"), P("ctx", "dp"), P("ctx", "dp"),
    )
    return jax.shard_map(
        functools.partial(per_device, nz, ndp), mesh=mesh, in_specs=specs,
        out_specs=(P("ctx", "dp"), P("ctx", "dp"), P("ctx", None), P("ctx", None)),
        check_vma=False,
    )
```

time: 78.8 us -> 70.9 us (0.90)
  local copies, waits for them, and re-layouts: 3.87 us -> 0 us
  Pallas kernels: 72.5 us -> 70.1 us
  other arithmetic: 1.36 us -> 0 us
    unnamed x14 -> x0, local copies, waits for them, and re-layouts: 3.87 us -> none
    pallas_call x1 -> x2, Pallas kernels: 72.5 us -> 70.1 us  [the longest x1 68.2 us: per_device(): pl.pallas_call(functools.partial(kernel, NZ, NDP), out_shape=shapes, in_s...]
where the time goes in v2:
time: 70.9 us; the launch traced here: 70.7 us
  Pallas kernels  70.1 us (99%)
    pallas_call x1, Pallas kernels, per_device(): pl.pallas_call(functools.partial(kernel, NZ, NDP), out_shape=shapes, in_s...  68.2 us
    pallas_call x1, Pallas kernels, per_device(): pl.pallas_call(write_out, out_shape=shapes, in_specs=[vmem] * 4, out_spec...  1.87 us

profile of v2, /device:TPU:1, one launch (start us, length us, event | category | flops | bytes accessed | tf_op | source)
XLA Modules:
  0.0 70.7 jit_solution(9994760267561464354)
XLA Ops:
  0.6 68.2 %distill.1 = (bf16[128,1024]{1,0:T(8,128)(2,1)}, bf16[128,1024]{1,0:T(8,128)(2,1)}, f32[16,512]{1,0:T(8,128)}, f32[16,512]{1,0:T(8,128)}) custom-call(bf16[128,1024]{1,0:T(8,128)(2,1)} %q_ref.1, bf16[128,128]{1,0:T(8,128)(2,1)} %k_hbm.1, bf16[128,128]{1,0:T(8,128)(2,1)} %v_hbm.1, s32[1,128]{1,0:T(1,128)} %bitcast.1, bf16[16,128]{1,0:T(8,128)(2,1)} %ck_hbm.1, ...), custom_call_target="tpu_custom_call" | custom-call | tf_op jit(solution)/shard_map/distill/pallas_call | solution.py:505
  68.8 1.9 %write_out.1 = (bf16[128,1024]{1,0:T(8,128)(2,1)}, bf16[128,1024]{1,0:T(8,128)(2,1)}, f32[16,512]{1,0:T(8,128)}, f32[16,512]{1,0:T(8,128)}) custom-call(bf16[128,1024]{1,0:T(8,128)(2,1)} %get-tuple-element.8.t_ref, bf16[128,1024]{1,0:T(8,128)(2,1)} %get-tuple-element.9.s_ref, f32[16,512]{1,0:T(8,128)} %get-tuple-element.10.gk_ref, ...), custom_call_target="tpu_custom_call" | custom-call | tf_op jit(solution)/shard_map/write_out/pallas_call | solution.py:546

commit v3 on v2

--- a/solution.py
+++ b/solution.py
@@ -15,6 +15,7 @@
 ROWS = 128
 PAIRS = 4
 WIDE = 256
+TILE = 256
 F32, BF16 = jnp.float32, jnp.bfloat16
 MESH = pl.DeviceIdType.MESH
 MASKED = -1e30
@@ -36,7 +37,7 @@
     q_ref, k_hbm, v_hbm, seg_hbm, ck_hbm, cv_hbm,
     t_out, s_out, gk_out, gv_out,
     kvbuf, segbuf, cartbuf, qrows, vt, ck, cv, cvt, m_ref, l_ref, acc, p_ref, plow, ot_ref,
-    delta_ref, row_ref, ds_ref,
+    delta_ref, row_ref, ds_ref, s_ref,
     sbuf, rbuf1, s2buf, rbuf2, gbuf, rs1, zbuf, rs2, fbuf, dbuf,
     loc_sem, send_sem, kvz_sem, kv_sem, seg_sem, segz_sem, cart_sem, cartz_sem,
     a1_sem, a2_sem, r1_sem, r2_sem, dp_sem,
@@ -273,32 +274,46 @@
             last = (q - c0) * ROWS + lax.broadcasted_iota(jnp.int32, (1, ROWS), 1)
             last = jnp.concatenate([last, last], axis=1)
             opening = k == 0 and c0 == 0
-
-            def pair(hp, carry):
-                heads = qrows[pl.ds(pl.multiple_of(hp * WIDE, WIDE), WIDE), :]
-                scores = dot_nt(key_rows, heads)
-                pos = lax.broadcasted_iota(jnp.int32, scores.shape, 0)
+            tiles = count * ROWS // TILE
+
+            def scores(hp, j, top):
+                part = dot_nt(key_rows[j * TILE:(j + 1) * TILE], qrows[hp * WIDE:(hp + 1) * WIDE, :])
+                pos = lax.broadcasted_iota(jnp.int32, part.shape, 0) + j * TILE
                 allowed = pos >= first
                 if k == 0:
                     allowed = allowed & (pos <= last)
-                scores = jnp.where(allowed, scores, MASKED)
-                top = jnp.max(scores, axis=0, keepdims=True)
+                part = jnp.where(allowed, part, MASKED)
+                s_ref[hp % 2, j * TILE:(j + 1) * TILE, :] = part
+                part = jnp.max(part.reshape(TILE // 8, 8, WIDE), axis=0)
+                return part if top is None else jnp.maximum(top, part)
+
+            top = None
+            for j in range(tiles):
+                top = scores(0, j, top)
+            for hp in range(PAIRS):
+                top = jnp.max(top, axis=0, keepdims=True)
                 if not opening:
                     old = m_ref[hp]
                     top = jnp.maximum(top, old)
                     factor = jnp.exp2((old - top) * EXP2_SCALE)
-                weights = jnp.exp2((scores - top) * EXP2_SCALE)
-                total = jnp.sum(weights, axis=0, keepdims=True)
-                mixed = dot_nn(vt[:, :count * ROWS], weights.astype(BF16))
+                total, mixed, ahead = None, None, None
+                for j in range(tiles):
+                    rows = slice(j * TILE, (j + 1) * TILE)
+                    weights = jnp.exp2((s_ref[hp % 2, rows, :] - top) * EXP2_SCALE)
+                    if hp + 1 < PAIRS:
+                        ahead = scores(hp + 1, j, ahead)
+                    part = jnp.sum(weights.reshape(TILE // 8, 8, WIDE), axis=0)
+                    total = part if total is None else total + part
+                    part = dot_nn(vt[:, rows], weights.astype(BF16))
+                    mixed = part if mixed is None else mixed + part
+                total = jnp.sum(total, axis=0, keepdims=True)
                 if not opening:
                     total = total + l_ref[hp] * factor
                     mixed = mixed + acc[hp] * factor
                 m_ref[hp] = top
                 l_ref[hp] = total
                 acc[hp] = mixed
-                return carry
-
-            lax.fori_loop(0, PAIRS, pair, 0)
+                top = ahead
 
         guarded(cond, body)
 
@@ -318,23 +333,51 @@
         cv[...] = cartbuf[:, :, 1].reshape(SL, HD)
         cvt[...] = dot_nt(eye, cv[...]).astype(BF16)
         swap = swap_matrix()
-        for hp in range(PAIRS):
-            cols = slice(hp * WIDE, (hp + 1) * WIDE)
-            logits = dot_nt(ck[...], qrows[cols, :])
-            top = jnp.max(logits, axis=0, keepdims=True)
-            expo = jnp.exp2((logits - top) * EXP2_SCALE)
-            total = jnp.sum(expo, axis=0, keepdims=True)
-            probs = expo * (1.0 / total)
+        tiles = SL // TILE
+
+        def logits(hp, j, top):
+            part = dot_nt(ck[j * TILE:(j + 1) * TILE, :], qrows[hp * WIDE:(hp + 1) * WIDE, :])
+            s_ref[hp % 2, j * TILE:(j + 1) * TILE, :] = part
+            part = jnp.max(part.reshape(TILE // 8, 8, WIDE), axis=0)
+            return part if top is None else jnp.maximum(top, part)
+
+        def probabilities(hp, j, inverse, out):
+            rows, cols = slice(j * TILE, (j + 1) * TILE), slice(hp * WIDE, (hp + 1) * WIDE)
+            probs = p_ref[rows, cols] * inverse
+            p_ref[rows, cols] = probs
             low = probs.astype(BF16)
-            p_ref[:, cols] = probs
-            plow[:, cols] = low
-            out = dot_nn(cvt[...], low)
-            ot_ref[:, cols] = out
-            out_low = out.astype(BF16)
-            for g in range(2):
-                h = hp * 2 + g
-                rows = dot_nt(swap, out_low[:, g * ROWS:(g + 1) * ROWS])
-                sbuf[:, :, h * HD:(h + 1) * HD] = rows.astype(BF16).reshape(NQ, 16, HD)
+            plow[rows, cols] = low
+            part = dot_nn(cvt[:, rows], low)
+            return part if out is None else out + part
+
+        top, inverse = None, None
+        for j in range(tiles):
+            top = logits(0, j, top)
+        for hp in range(PAIRS + 1):
+            if hp < PAIRS:
+                top = jnp.max(top, axis=0, keepdims=True)
+            total, ahead, out = None, None, None
+            for j in range(tiles):
+                rows, cols = slice(j * TILE, (j + 1) * TILE), slice(hp * WIDE, (hp + 1) * WIDE)
+                if hp < PAIRS:
+                    expo = jnp.exp2((s_ref[hp % 2, rows, :] - top) * EXP2_SCALE)
+                    p_ref[rows, cols] = expo
+                    part = jnp.sum(expo.reshape(TILE // 8, 8, WIDE), axis=0)
+                    total = part if total is None else total + part
+                if hp + 1 < PAIRS:
+                    ahead = logits(hp + 1, j, ahead)
+                if hp > 0:
+                    out = probabilities(hp - 1, j, inverse, out)
+            if hp > 0:
+                ot_ref[:, (hp - 1) * WIDE:hp * WIDE] = out
+                out_low = out.astype(BF16)
+                for g in range(2):
+                    h = (hp - 1) * 2 + g
+                    rows = dot_nt(swap, out_low[:, g * ROWS:(g + 1) * ROWS])
+                    sbuf[:, :, h * HD:(h + 1) * HD] = rows.astype(BF16).reshape(NQ, 16, HD)
+            if hp < PAIRS:
+                inverse = 1.0 / jnp.sum(total, axis=0, keepdims=True)
+            top = ahead
 
     def exchange1():
         for r in range(1, NQ):
@@ -451,11 +494,11 @@
     have(1, round1)
     have(3, z_recv)
     have(3, round0)
+    have(4, z_recv)
+    have(4, round0)
     round2(0)
     teach(0)
     have(2, round1)
-    have(4, z_recv)
-    have(4, round0)
     have(1, round2)
     have(1, teach)
     have(3, round1)
@@ -463,10 +506,12 @@
     student()
     have(4, round1)
     exchange1()
-    for k in (2, 3, 4):
+    for k in (2, 3):
         have(k, round2)
         have(k, teach)
+    have(4, round2)
     exchange2()
+    have(4, teach)
     difference()
     gradients(0)
     reduce1(0)
@@ -525,6 +570,7 @@
             V((HD, 1024), BF16),
             V((1, 1024), F32),
             V((SL // 2, 1024), BF16),
+            V((2, NQ * ROWS, WIDE), F32),
             V((NQ, 16, 1024), BF16),
             V((NQ, 16, 1024), BF16),
             V((NQ, 16, 1024), BF16),

time: 70.9 us -> 63.1 us (0.89)
  Pallas kernels: 70.1 us -> 62.1 us
    pallas_call x1, Pallas kernels: 68.2 us -> 60.2 us  [per_device(): pl.pallas_call(functools.partial(kernel, NZ, NDP), out_shape=shapes, in_s...]
where the time goes in v3:
time: 63.1 us; the launch traced here: 62.9 us
  Pallas kernels  62.1 us (98%)
  between operations  0.8 us (1%)
    pallas_call x1, Pallas kernels, per_device(): pl.pallas_call(functools.partial(kernel, NZ, NDP), out_shape=shapes, in_s...  60.2 us
    pallas_call x1, Pallas kernels, per_device(): pl.pallas_call(write_out, out_shape=shapes, in_specs=[vmem] * 4, out_spec...  1.87 us

profile of v3, /device:TPU:1, one launch (start us, length us, event | category | flops | bytes accessed | tf_op | source)
XLA Modules:
  0.0 62.9 jit_solution(16775806183768388383)
XLA Ops:
  0.6 60.2 %distill.1 = (bf16[128,1024]{1,0:T(8,128)(2,1)}, bf16[128,1024]{1,0:T(8,128)(2,1)}, f32[16,512]{1,0:T(8,128)}, f32[16,512]{1,0:T(8,128)}) custom-call(bf16[128,1024]{1,0:T(8,128)(2,1)} %q_ref.1, bf16[128,128]{1,0:T(8,128)(2,1)} %k_hbm.1, bf16[128,128]{1,0:T(8,128)(2,1)} %v_hbm.1, s32[1,128]{1,0:T(1,128)} %bitcast.1, bf16[16,128]{1,0:T(8,128)(2,1)} %ck_hbm.1, ...), custom_call_target="tpu_custom_call" | custom-call | tf_op jit(solution)/shard_map/distill/pallas_call | solution.py:550
  60.9 1.9 %write_out.1 = (bf16[128,1024]{1,0:T(8,128)(2,1)}, bf16[128,1024]{1,0:T(8,128)(2,1)}, f32[16,512]{1,0:T(8,128)}, f32[16,512]{1,0:T(8,128)}) custom-call(bf16[128,1024]{1,0:T(8,128)(2,1)} %get-tuple-element.8.t_ref, bf16[128,1024]{1,0:T(8,128)(2,1)} %get-tuple-element.9.s_ref, f32[16,512]{1,0:T(8,128)} %get-tuple-element.10.gk_ref, ...), custom_call_target="tpu_custom_call" | custom-call | tf_op jit(solution)/shard_map/write_out/pallas_call | solution.py:592

commit v4 on v3

--- a/solution.py
+++ b/solution.py
@@ -34,10 +34,10 @@
 
 def kernel(
     NZ, NDP,
-    q_ref, k_hbm, v_hbm, seg_hbm, ck_hbm, cv_hbm,
+    q_hbm, k_hbm, v_hbm, seg_hbm, ck_hbm, cv_hbm,
     t_out, s_out, gk_out, gv_out,
     kvbuf, segbuf, cartbuf, qrows, vt, ck, cv, cvt, m_ref, l_ref, acc, p_ref, plow, ot_ref,
-    delta_ref, row_ref, ds_ref, s_ref,
+    delta_ref, row_ref, ds_ref, s_ref, low_ref,
     sbuf, rbuf1, s2buf, rbuf2, gbuf, rs1, zbuf, rs2, fbuf, dbuf,
     loc_sem, send_sem, kvz_sem, kv_sem, seg_sem, segz_sem, cart_sem, cartz_sem,
     a1_sem, a2_sem, r1_sem, r2_sem, dp_sem,
@@ -65,6 +65,7 @@
             pl.when(cond())(body)
 
     sent = []
+    done = [0]
 
     def send(refs, to, cond=None):
         slot = len(sent)
@@ -90,11 +91,13 @@
 
         guarded(cond, body)
 
+    near = [r for r in ((1, -1, 2, -2) if NZ >= 8 else range(1, NZ))]
+
     barrier = pltpu.get_barrier_semaphore()
 
     def greet():
         for r in range(1, NZ):
-            pl.semaphore_signal(barrier, 1, device_id=(ctx(z + r, q), d), device_id_type=MESH)
+            pl.semaphore_signal(barrier, 1, device_id=(ctx(z + r + NZ, q), d), device_id_type=MESH)
         for r in range(1, NDP):
             pl.semaphore_signal(barrier, 1, device_id=(me, rem(d + r, NDP)), device_id_type=MESH)
         for r in range(1, NQ):
@@ -109,6 +112,12 @@
             pltpu.make_async_copy(cv_hbm, cartbuf.at[z, q, 1], loc_sem.at[4]),
         ]
 
+    def query_copies():
+        return [
+            pltpu.make_async_copy(q_hbm.at[:, pl.ds(h * HD, HD)], qrows.at[pl.ds(h * ROWS, ROWS)], loc_sem.at[5 + h])
+            for h in range(8)
+        ]
+
     def seg_start():
         for r in range(1, NQ):
             send(lambda: (segbuf.at[0, q], segbuf.at[0, q], seg_sem.at[q]),
@@ -117,12 +126,18 @@
     def seg_spread():
         for r in range(1, NQ):
             recv(lambda r=r: (segbuf.at[0, rem(q + r, NQ)], seg_sem.at[rem(q + r, NQ)]))
-        for k in range(1, NP):
+        for k in range(1, min(NP, 3)):
             send(lambda k=k: (segbuf.at[0], segbuf.at[k], segz_sem.at[k]),
                  lambda k=k: (ctx(z + k, q), d), lambda k=k: z + k < NZ)
 
+    def seg_relay():
+        recv(lambda: (segbuf.at[2], segz_sem.at[2]), lambda: z >= 2)
+        for k in range(3, NP):
+            send(lambda k=k: (segbuf.at[2], segbuf.at[k], segz_sem.at[k]),
+                 lambda k=k: (ctx(z + k - 2, q), d), lambda k=k: (z >= 2) & (z + k - 2 < NZ))
+
     def seg_wait(k):
-        if k > 0:
+        if k > 0 and k != 2:
             recv(lambda: (segbuf.at[k], segz_sem.at[k]), lambda: z >= k)
 
     def plane(r):
@@ -133,7 +148,6 @@
             send(lambda: (cartbuf.at[z, q], cartbuf.at[z, q], cart_sem.at[q]),
                  lambda r=r: (ctx(z, rem(q + r, NQ)), d))
 
-    near = [r for r in ((1, -1, 2, -2) if NZ >= 8 else range(1, NZ))]
 
     def cart_spread():
         for r in range(1, NQ):
@@ -166,7 +180,7 @@
             recv(lambda p=p: (cartbuf.at[plane(4), pl.ds(p * 4, 4)], cartz_sem.at[plane(4), p]))
 
     CUT = 96
-    LOW, HIGH = (0, CUT), (CUT, 2 * ROWS - CUT)
+    LOW, HIGH, ALL = (0, CUT), (CUT, 2 * ROWS - CUT), (0, 2 * ROWS)
 
     def piece(k, qq, part):
         return kvbuf.at[k, qq, pl.ds(part[0], part[1])]
@@ -182,12 +196,12 @@
         return None if k == 0 else (lambda: z >= k)
 
     def hand(k, src, dst, part, cond):
-        i = 0 if part is LOW else 1
+        i = 1 if part is HIGH else 0
         send(lambda: (piece(k, src(), part), piece(k, src(), part), kv_sem.at[k, src(), i]),
              lambda: (ctx(z, dst()), d), cond)
 
     def take(k, src, part, cond):
-        i = 0 if part is LOW else 1
+        i = 1 if part is HIGH else 0
         recv(lambda: (piece(k, src(), part), kv_sem.at[k, src(), i]), cond)
 
     home = lambda: q
@@ -200,11 +214,23 @@
     def z_recv(k):
         recv(lambda: (kvbuf.at[k, q], kvz_sem.at[k]), lambda: z >= k)
         if k == 2:
-            for steps in (1, 2):
+            for steps in (1,):
                 if k + steps < NP:
                     z_send(k, steps)
 
+    def direct(k):
+        for dx, flip in ((2, True), (2, False), (1, True), (3, True), (1, False), (3, False), (0, True)):
+            there = lambda dx=dx, flip=flip: at(dx, flip)
+            hand(k, home, there, ALL, need(k, home, there))
+
+    def direct_wait(k):
+        for dx, flip in ((0, True), (1, False), (3, False), (1, True), (3, True), (2, False), (2, True)):
+            source = lambda dx=dx, flip=flip: at(dx, flip)
+            take(k, source, ALL, need(k, source, home))
+
     def round0(k):
+        if k == 4:
+            return direct(k)
         hand(k, home, twin, LOW, exists(k))
         for dx in (2, 1, 3):
             there = lambda dx=dx: at(dx, False)
@@ -215,6 +241,8 @@
         hand(k, home, twin, HIGH, need(k, home, twin))
 
     def round1(k):
+        if k == 4:
+            return
         take(k, twin, LOW, exists(k))
         for dx in (2, 1, 3):
             there = lambda dx=dx: at(dx, False)
@@ -225,6 +253,8 @@
             hand(k, source, twin, HIGH, need(k, source, twin))
 
     def round2(k):
+        if k == 4:
+            return direct_wait(k)
         for dx in (1, 3, 2):
             for flip in (False, True):
                 source = lambda dx=dx, flip=flip: at(dx, flip)
@@ -245,8 +275,6 @@
         return (src == j).astype(F32).astype(BF16)
 
     def prepare():
-        for h in range(8):
-            qrows[h * ROWS:(h + 1) * ROWS, :] = q_ref[:, h * HD:(h + 1) * HD]
         for s in range(NQ):
             @pl.when(s > q)
             def _():
@@ -408,9 +436,11 @@
             delta = (WEIGHT * (out - low_t.astype(F32))).astype(BF16)
             delta_ref[:, cols] = delta
             row_ref[:, cols] = jnp.sum(delta.astype(F32) * out, axis=0, keepdims=True)
-            for g in range(2):
-                h = hp * 2 + g
-                t_out[:, h * HD:(h + 1) * HD] = dot_nt(eye, low_t[:, g * ROWS:(g + 1) * ROWS]).astype(BF16)
+            low_ref[:, cols] = low_t
+
+    def teacher_rows():
+        for h in range(8):
+            t_out[:, h * HD:(h + 1) * HD] = dot_nt(eye, low_ref[:, h * ROWS:(h + 1) * ROWS]).astype(BF16)
 
     NH = 2
     HZ = NZ // NH
@@ -464,33 +494,41 @@
             gk_out[:, s * HD:(s + 1) * HD] = dbuf[s, 0]
             gv_out[:, s * HD:(s + 1) * HD] = dbuf[s, 1]
 
-    def finish():
-        for cond, make in sent:
+    def finish(upto=None):
+        upto = len(sent) if upto is None else upto
+        for cond, make in sent[done[0]:upto]:
             guarded(cond, lambda: make().wait_send())
+        done[0] = upto
 
     have = lambda k, part: part(k) if k < NP else None
     greet()
     own = own_copies()
     for c in own:
         c.start()
+    asked = query_copies()
+    for c in asked:
+        c.start()
     prepare()
     for c in own:
         c.wait()
     pl.semaphore_wait(barrier, NQ - 1 + NZ - 1 + NDP - 1)
-    z_send(0, 1)
-    if NP > 2:
-        z_send(0, 2)
+    for steps in (1, 2, 4):
+        if steps < NP:
+            z_send(0, steps)
     seg_start()
     cart_start()
     round0(0)
+    for c in asked:
+        c.wait()
     seg_spread()
-    cart_spread()
     have(1, z_recv)
     have(1, round0)
-    round1(0)
     have(2, z_recv)
     have(2, round0)
-    cart_relay()
+    cart_spread()
+    round1(0)
+    if NP > 2:
+        seg_relay()
     have(1, round1)
     have(3, z_recv)
     have(3, round0)
@@ -499,24 +537,25 @@
     round2(0)
     teach(0)
     have(2, round1)
+    cart_relay()
     have(1, round2)
     have(1, teach)
     have(3, round1)
     cart_wait()
     student()
-    have(4, round1)
     exchange1()
-    for k in (2, 3):
+    for k in (2, 3, 4):
         have(k, round2)
         have(k, teach)
-    have(4, round2)
-    exchange2()
-    have(4, teach)
+    early = len(sent)
     difference()
     gradients(0)
     reduce1(0)
     gradients(1)
     reduce1(1)
+    exchange2()
+    teacher_rows()
+    finish(early)
     reduce2(0)
     reduce2(1)
     reduce3()
@@ -549,8 +588,8 @@
     ]
     results = pl.pallas_call(
         functools.partial(kernel, NZ, NDP),
-        out_shape=shapes,
-        in_specs=[vmem, hbm, hbm, hbm, hbm, hbm],
+        out_shape=[pltpu.VMEM(a.shape, a.dtype) for a in shapes],
+        in_specs=[hbm] * 6,
         out_specs=[vmem] * 4,
         scratch_shapes=[
             V((NP, NQ, 2 * ROWS, HD), BF16),
@@ -571,6 +610,7 @@
             V((1, 1024), F32),
             V((SL // 2, 1024), BF16),
             V((2, NQ * ROWS, WIDE), F32),
+            V((HD, 1024), BF16),
             V((NQ, 16, 1024), BF16),
             V((NQ, 16, 1024), BF16),
             V((NQ, 16, 1024), BF16),
@@ -581,7 +621,7 @@
             V((NZ, 2, 16, HD), BF16),
             V((2, 16, HD), F32),
             V((NDP, 2, 16, HD), F32),
-            D((5,)), D((160,)), D((NP,)), D((NP, NQ, 2)), D((NQ,)), D((NP,)), D((NQ,)), D((NZ, 2)),
+            D((13,)), D((160,)), D((NP,)), D((NP, NQ, 2)), D((NQ,)), D((NP,)), D((NQ,)), D((NZ, 2)),
             D((NQ,)), D((NZ,)), D((NQ, 2)), D((NZ,)), D((NDP,)),
         ],
         compiler_params=pltpu.CompilerParams(
@@ -589,6 +629,7 @@
         ),
         name="distill",
     )(queries, keys, values, segment_ids.reshape(1, ROWS), cart_keys, cart_values)
+    results = [pltpu.with_memory_space_constraint(a, pltpu.VMEM) for a in results]
     return pl.pallas_call(
         write_out, out_shape=shapes, in_specs=[vmem] * 4, out_specs=[hbm] * 4,
         scratch_shapes=[D((4,))], name="write_out",

time: 63.1 us -> 59.7 us (0.946)
  Pallas kernels: 62.1 us -> 58.8 us
    pallas_call x1, Pallas kernels: 60.2 us -> 58 us  [per_device(): pl.pallas_call(functools.partial(kernel, NZ, NDP), out_shape=[pltpu.VMEM(...]
    pallas_call x1, Pallas kernels: 1.87 us -> 0.84 us  [per_device(): pl.pallas_call(write_out, out_shape=shapes, in_specs=[vmem] * 4, out_spec...]
where the time goes in v4:
time: 59.7 us; the launch traced here: 59.6 us
  Pallas kernels  58.8 us (98%)
  between operations  0.8 us (1%)
    pallas_call x1, Pallas kernels, per_device(): pl.pallas_call(functools.partial(kernel, NZ, NDP), out_shape=[pltpu.VMEM(...  58 us

profile of v4, /device:TPU:1, one launch (start us, length us, event | category | flops | bytes accessed | tf_op | source)
XLA Modules:
  0.0 59.6 jit_solution(1782483653550575698)
XLA Ops:
  0.6 58.0 %distill.1 = (bf16[128,1024]{1,0:T(8,128)(2,1)S(1)}, bf16[128,1024]{1,0:T(8,128)(2,1)S(1)}, f32[16,512]{1,0:T(8,128)S(1)}, f32[16,512]{1,0:T(8,128)S(1)}) custom-call(bf16[128,1024]{1,0:T(8,128)(2,1)} %q_hbm.1, bf16[128,128]{1,0:T(8,128)(2,1)} %k_hbm.1, bf16[128,128]{1,0:T(8,128)(2,1)} %v_hbm.1, s32[1,128]{1,0:T(1,128)} %bitcast.1, bf16[16,128]{1,0:T(8,128)(2,1)} %ck_hbm.1, ...), custom_call_target="tpu_custom_call" | custom-call | tf_op jit(solution)/shard_map/distill/pallas_call | solution.py:589
  58.6 0.8 %write_out.1 = (bf16[128,1024]{1,0:T(8,128)(2,1)}, bf16[128,1024]{1,0:T(8,128)(2,1)}, f32[16,512]{1,0:T(8,128)}, f32[16,512]{1,0:T(8,128)}) custom-call(bf16[128,1024]{1,0:T(8,128)(2,1)S(1)} %get-tuple-element.8.t_ref, bf16[128,1024]{1,0:T(8,128)(2,1)S(1)} %get-tuple-element.9.s_ref, f32[16,512]{1,0:T(8,128)S(1)} %get-tuple-element.10.gk_ref, ...), custom_call_target="tpu_custom_call" | custom-call | tf_op jit(solution)/shard_map/write_out/pallas_call | solution.py:633

commit v5 on v4

--- a/solution.py
+++ b/solution.py
@@ -96,7 +96,7 @@
     barrier = pltpu.get_barrier_semaphore()
 
     def greet():
-        for r in range(1, NZ):
+        for r in near:
             pl.semaphore_signal(barrier, 1, device_id=(ctx(z + r + NZ, q), d), device_id_type=MESH)
         for r in range(1, NDP):
             pl.semaphore_signal(barrier, 1, device_id=(me, rem(d + r, NDP)), device_id_type=MESH)
@@ -214,7 +214,7 @@
     def z_recv(k):
         recv(lambda: (kvbuf.at[k, q], kvz_sem.at[k]), lambda: z >= k)
         if k == 2:
-            for steps in (1,):
+            for steps in (1, 2):
                 if k + steps < NP:
                     z_send(k, steps)
 
@@ -511,8 +511,8 @@
     prepare()
     for c in own:
         c.wait()
-    pl.semaphore_wait(barrier, NQ - 1 + NZ - 1 + NDP - 1)
-    for steps in (1, 2, 4):
+    pl.semaphore_wait(barrier, NQ - 1 + len(near) + NDP - 1)
+    for steps in (1, 2):
         if steps < NP:
             z_send(0, steps)
     seg_start()

time: 59.7 us -> 59.1 us (0.990)
  Pallas kernels: 58.8 us -> 58.1 us
    pallas_call x1, Pallas kernels: 58 us -> 57.3 us  [per_device(): pl.pallas_call(functools.partial(kernel, NZ, NDP), out_shape=[pltpu.VMEM(...]
where the time goes in v5:
time: 59.1 us; the launch traced here: 58.9 us
  Pallas kernels  58.1 us (98%)
  between operations  0.8 us (1%)
    pallas_call x1, Pallas kernels, per_device(): pl.pallas_call(functools.partial(kernel, NZ, NDP), out_shape=[pltpu.VMEM(...  57.3 us

profile of v5, /device:TPU:1, one launch (start us, length us, event | category | flops | bytes accessed | tf_op | source)
XLA Modules:
  0.0 58.9 jit_solution(5323787745092609423)
XLA Ops:
  0.6 57.3 %distill.1 = (bf16[128,1024]{1,0:T(8,128)(2,1)S(1)}, bf16[128,1024]{1,0:T(8,128)(2,1)S(1)}, f32[16,512]{1,0:T(8,128)S(1)}, f32[16,512]{1,0:T(8,128)S(1)}) custom-call(bf16[128,1024]{1,0:T(8,128)(2,1)} %q_hbm.1, bf16[128,128]{1,0:T(8,128)(2,1)} %k_hbm.1, bf16[128,128]{1,0:T(8,128)(2,1)} %v_hbm.1, s32[1,128]{1,0:T(1,128)} %bitcast.1, bf16[16,128]{1,0:T(8,128)(2,1)} %ck_hbm.1, ...), custom_call_target="tpu_custom_call" | custom-call | tf_op jit(solution)/shard_map/distill/pallas_call | solution.py:589
  58.0 0.8 %write_out.1 = (bf16[128,1024]{1,0:T(8,128)(2,1)}, bf16[128,1024]{1,0:T(8,128)(2,1)}, f32[16,512]{1,0:T(8,128)}, f32[16,512]{1,0:T(8,128)}) custom-call(bf16[128,1024]{1,0:T(8,128)(2,1)S(1)} %get-tuple-element.8.t_ref, bf16[128,1024]{1,0:T(8,128)(2,1)S(1)} %get-tuple-element.9.s_ref, f32[16,512]{1,0:T(8,128)S(1)} %get-tuple-element.10.gk_ref, ...), custom_call_target="tpu_custom_call" | custom-call | tf_op jit(solution)/shard_map/write_out/pallas_call | solution.py:633
